TPU v7x, 32 devices: a whole 2x2x4 slice. The times are simulated.
32 devices in a mesh: dp: 2 (over x), expert: 16 (over z, y, core).
Axes of the slice: x: 2, y: 2, z: 4, core: 2. Of those that a mesh axis runs over, the one named last changes fastest.
Arguments:
- tokens: bfloat16 [2048, 2560], P('expert', 'dp'), may hold values from -6 to 6
- cotangent: bfloat16 [2048, 2560], P('expert', 'dp'), may hold values from -6 to 6
- expert_ids: int32 [2048, 6], P('expert'), may hold values from 0 to 15, all different within a row; in each aligned block of 128 rows (0 to 127, 128 to 255, ...) at most 64 rows name the same one
- gate_weights: float32 [2048, 6], P('expert'), may hold values from 0.1 to 0.6
- w_in: bfloat16 [16, 2560, 768], P('expert', 'dp'), may hold values from -0.125 to 0.125
- w_out: bfloat16 [16, 768, 2560], P('expert', None, 'dp'), may hold values from -0.21875 to 0.21875
Outputs:
- mixed_out: bfloat16 [2048, 2560], P('expert', 'dp')
- token_grad: bfloat16 [2048, 2560], P('expert', 'dp')
- w_in_grad: bfloat16 [16, 2560, 768], P('expert', 'dp')
- w_out_grad: bfloat16 [16, 768, 2560], P('expert', None, 'dp')
Inputs may be any that keep to these rules, and one draw needn't show every extreme that they name: `expert_ids`: each row names 6 different experts. Within the rows of one device (aligned blocks of 128 rows) no expert is named more than 64 times, a bound that some block reaches.
All inputs are finite; a program needn't handle non-finite values.
Results may differ from a plain program's by a relative error of at most 0.017.
Values may be sent and summed in bfloat16 or wider, within the bound.
A program may use at most 64 MiB of HBM per device.

v0:
```python
import jax
import jax.numpy as jnp
from jax import lax
from jax.sharding import PartitionSpec as P


def silu_slope(hidden_value):
    logistic = jax.nn.sigmoid(hidden_value)
    return logistic * (1.0 + hidden_value * (1.0 - logistic))


def expert_hidden(rows_x, weight_in):
    partial_sum = jnp.dot(rows_x, weight_in, preferred_element_type=jnp.float32)
    share_sum = lax.psum_scatter(
        partial_sum.astype(jnp.bfloat16), "dp", scatter_dimension=1, tiled=True
    ).astype(jnp.float32)
    share_act = jax.nn.silu(share_sum).astype(jnp.bfloat16)
    return (share_sum, lax.all_gather(share_act, "dp", axis=1, tiled=True))


def expert_slope(rows_dy, weight_out, preact):
    partial_sum = lax.dot_general(
        rows_dy, weight_out, (((1,), (1,)), ((), ())), preferred_element_type=jnp.float32
    )
    share_sum = lax.psum_scatter(
        partial_sum.astype(jnp.bfloat16), "dp", scatter_dimension=1, tiled=True
    ).astype(jnp.float32)
    share_delta = (share_sum * silu_slope(preact)).astype(jnp.bfloat16)
    return lax.all_gather(share_delta, "dp", axis=1, tiled=True)


def local(tokens, cotangent, expert_ids, gate_weights, w_in, w_out):
    experts = lax.axis_size("expert")
    tok_rows, quarter = tokens.shape
    choose_count = expert_ids.shape[1]
    capacity = max(2, 4 * tok_rows * choose_count // (3 * experts))
    assign = tok_rows * choose_count
    flat_ids = expert_ids.reshape(-1)
    onehot = (flat_ids[:, None] == jnp.arange(experts, dtype=jnp.int32)[None, :]).astype(jnp.int32)
    earlier = jnp.sum((jnp.cumsum(onehot, axis=0) - onehot) * onehot, axis=1)
    slot_index = flat_ids * capacity + earlier
    source = (
        jnp.full((experts * capacity,), assign, jnp.int32)
        .at[slot_index]
        .set(jnp.arange(assign, dtype=jnp.int32))
    )
    token_of = source // choose_count
    zero_row = jnp.zeros((1, quarter), jnp.bfloat16)
    send_x = jnp.concatenate([tokens, zero_row], 0)[token_of].reshape(experts, capacity, quarter)
    slot_gate = jnp.concatenate([gate_weights.reshape(-1), jnp.zeros((1,), jnp.float32)], 0)[source]
    picked_dy = jnp.concatenate([cotangent, zero_row], 0)[token_of]
    send_dy = (
        (slot_gate[:, None] * picked_dy.astype(jnp.float32))
        .astype(jnp.bfloat16)
        .reshape(experts, capacity, quarter)
    )
    weight_in = w_in[0]
    weight_out = w_out[0]
    arrived_x = lax.all_to_all(send_x, "expert", split_axis=0, concat_axis=0, tiled=True)
    rows_x = arrived_x.reshape(-1, quarter)
    preact, activation = expert_hidden(rows_x, weight_in)
    out_rows = jnp.dot(activation, weight_out, preferred_element_type=jnp.float32).astype(
        jnp.bfloat16
    )
    rows_x, preact, activation, out_rows = (
        rows_x,
        preact,
        activation,
        out_rows.reshape(experts, capacity, quarter),
    )
    returned_out = lax.all_to_all(out_rows, "expert", split_axis=0, concat_axis=0, tiled=True)
    arrived_dy = lax.all_to_all(send_dy, "expert", split_axis=0, concat_axis=0, tiled=True)
    rows_dy = arrived_dy.reshape(-1, quarter)
    delta_hidden = expert_slope(rows_dy, weight_out, preact)
    out_grad = lax.dot_general(
        activation, rows_dy, (((0,), (0,)), ((), ())), preferred_element_type=jnp.float32
    ).astype(jnp.bfloat16)
    in_grad = lax.dot_general(
        rows_x, delta_hidden, (((0,), (0,)), ((), ())), preferred_element_type=jnp.float32
    ).astype(jnp.bfloat16)
    back_rows = lax.dot_general(
        delta_hidden, weight_in, (((1,), (1,)), ((), ())), preferred_element_type=jnp.float32
    ).astype(jnp.bfloat16)
    in_grad, out_grad, back_rows = (
        in_grad[None],
        out_grad[None],
        back_rows.reshape(experts, capacity, quarter),
    )
    returned_back = lax.all_to_all(back_rows, "expert", split_axis=0, concat_axis=0, tiled=True)

    def gather_rows(returned):
        flat_rows = returned.reshape(experts * capacity, quarter)
        return flat_rows[slot_index].astype(jnp.float32).reshape(tok_rows, choose_count, quarter)

    mixed_out = jnp.sum(gather_rows(returned_out) * gate_weights[:, :, None], axis=1).astype(
        jnp.bfloat16
    )
    token_grad = jnp.sum(gather_rows(returned_back), axis=1).astype(jnp.bfloat16)
    return (mixed_out, token_grad, in_grad, out_grad)


def solution(mesh):
    in_specs = (
        P("expert", "dp"),
        P("expert", "dp"),
        P("expert", None),
        P("expert", None),
        P("expert", "dp", None),
        P("expert", None, "dp"),
    )
    out_specs = (
        P("expert", "dp"),
        P("expert", "dp"),
        P("expert", "dp", None),
        P("expert", None, "dp"),
    )
    return jax.shard_map(local, mesh=mesh, in_specs=in_specs, out_specs=out_specs, check_vma=False)
```

profile of v0, /device:TPU:13, one launch (start us, length us, event | category | flops | bytes accessed | tf_op | source)
XLA Modules:
  0.0 386.5 jit_solution(10710059806611601516)
XLA Ops:
  15.9 4.5 %gather_fusion.2 = f32[1024]{0:T(1024)S(1)} fusion(f32[769]{0:T(1024)S(1)} %pad_maximum_fusion, s32[1024]{0:T(1024)S(1)} %get-tuple-element.6), kind=kCustom, calls=%fused_computation.2 | custom fusion | bytes 12288 | tf_op jit(solution)/shard_map/gather | solution.py:50
  20.5 5.5 %gather_fusion.3 = bf16[1024,1280]{1,0:T(8,128)(2,1)} fusion(bf16[129,1280]{1,0:T(8,128)(2,1)S(1)} %concatenate.11, s32[1024]{0:T(1024)S(1)} %get-tuple-element.7), kind=kCustom, calls=%fused_computation.3 | custom fusion | bytes 5246976 | tf_op jit(solution)/shard_map/gather | solution.py:51
  29.8 6.7 %all-to-all-start.2 = ((bf16[16,64,1280]{2,1,0:T(8,128)(2,1)}), bf16[16,64,1280]{2,1,0:T(8,128)(2,1)}, u32[]{:S(2)}, u32[]{:S(2)}) async-start(bf16[16,64,1280]{2,1,0:T(8,128)(2,1)} %fusion), calls=%async_computation.2 | async-start | bytes 5242880 | tf_op jit(solution)/shard_map/all_to_all | solution.py:72
  36.4 5.5 %gather_fusion = bf16[1024,1280]{1,0:T(8,128)(2,1)} fusion(bf16[129,1280]{1,0:T(8,128)(2,1)S(1)} %concatenate.9, s32[1024]{0:T(1024)S(1)} %get-tuple-element.7), kind=kCustom, calls=%fused_computation | custom fusion | bytes 5246976 | tf_op jit(solution)/shard_map/gather | solution.py:49
  41.9 53.3 %all-to-all-done.2 = bf16[16,64,1280]{2,1,0:T(8,128)(2,1)} async-done(((bf16[16,64,1280]{2,1,0:T(8,128)(2,1)}), bf16[16,64,1280]{2,1,0:T(8,128)(2,1)}, u32[]{:S(2)}, u32[]{:S(2)}) %all-to-all-start.2) | async-done | bytes 2621472 | tf_op jit(solution)/shard_map/all_to_all | solution.py:72
  95.2 4.8 %all-to-all-start = ((bf16[16,64,1280]{2,1,0:T(8,128)(2,1)}), bf16[16,64,1280]{2,1,0:T(8,128)(2,1)}, u32[]{:S(2)}, u32[]{:S(2)}) async-start(bf16[16,64,1280]{2,1,0:T(8,128)(2,1)} %bitcast.60), calls=%async_computation | async-start | bytes 5242880 | tf_op jit(solution)/shard_map/all_to_all | solution.py:59
  105.7 53.0 %all-to-all-done = bf16[16,64,1280]{2,1,0:T(8,128)(2,1)} async-done(((bf16[16,64,1280]{2,1,0:T(8,128)(2,1)}), bf16[16,64,1280]{2,1,0:T(8,128)(2,1)}, u32[]{:S(2)}, u32[]{:S(2)}) %all-to-all-start) | async-done | bytes 2621472 | tf_op jit(solution)/shard_map/all_to_all | solution.py:59
  158.7 4.5 %fusion.9 = bf16[1024,768]{1,0:T(8,128)(2,1)S(1)} fusion(bf16[1024,1280]{1,0:T(8,128)(2,1)} %bitcast.2, bf16[1,1280,768]{2,1,0:T(8,128)(2,1)} %param.10), kind=kOutput, calls=%fused_computation.24 | convolution fusion | flops 2014052352 | bytes 6160384 | tf_op jit(solution)/shard_map/dot_general | solution.py:13
  166.5 24.0 %reduce-scatter.7.cloned.1.call-done = bf16[384,1024]{1,0:T(8,128)(2,1)} async-done(((bf16[768,1024]{1,0:T(8,128)(2,1)}), bf16[384,1024]{1,0:T(8,128)(2,1)}) %reduce-scatter.7.cloned.1.call-update) | async-done | bytes 786448
  193.8 27.4 %all-gather.3.cloned.1.call-done = bf16[1024,768]{1,0:T(8,128)(2,1)} async-done(((bf16[1024,384]{1,0:T(8,128)(2,1)}), bf16[1024,768]{1,0:T(8,128)(2,1)}) %all-gather.3.cloned.1.call-update) | async-done | bytes 1572880 | tf_op jit(solution)/shard_map/all_gather | solution.py:18
  221.2 5.2 %convolution_convert_fusion.1 = bf16[1024,1280]{1,0:T(8,128)(2,1)} fusion(bf16[1024,768]{1,0:T(8,128)(2,1)} %all-gather.3.cloned.1.call-done, bf16[1,768,1280]{2,1,0:T(8,128)(2,1)S(1)} %copy-done), kind=kOutput, calls=%fused_computation.10 | convolution fusion | flops 2014576640 | bytes 6160384 | tf_op jit(solution)/shard_map/dot_general | solution.py:62
  226.4 6.5 %all-to-all-start.1 = ((bf16[16,64,1280]{2,1,0:T(8,128)(2,1)}), bf16[16,64,1280]{2,1,0:T(8,128)(2,1)}, u32[]{:S(2)}, u32[]{:S(2)}) async-start(bf16[16,64,1280]{2,1,0:T(8,128)(2,1)} %bitcast.64), calls=%async_computation.1 | async-start | bytes 5242880 | tf_op jit(solution)/shard_map/all_to_all | solution.py:71
  233.4 28.8 %all-gather.5.cloned.1.call-done = bf16[1024,768]{1,0:T(8,128)(2,1)} async-done(((bf16[1024,384]{1,0:T(8,128)(2,1)}), bf16[1024,768]{1,0:T(8,128)(2,1)}) %all-gather.5.cloned.1.call-update) | async-done | bytes 1572880 | tf_op jit(solution)/shard_map/all_gather | solution.py:29
  262.2 5.8 %convolution_convert_fusion = bf16[1024,1280]{1,0:T(8,128)(2,1)} fusion(bf16[1024,768]{1,0:T(8,128)(2,1)} %all-gather.5.cloned.1.call-done, bf16[1,1280,768]{2,1,0:T(8,128)(2,1)} %param.10), kind=kOutput, calls=%fused_computation.9 | convolution fusion | flops 2014576640 | bytes 6160384 | tf_op jit(solution)/shard_map/dot_general | solution.py:81
  268.0 23.6 %all-to-all-done.1 = bf16[16,64,1280]{2,1,0:T(8,128)(2,1)} async-done(((bf16[16,64,1280]{2,1,0:T(8,128)(2,1)}), bf16[16,64,1280]{2,1,0:T(8,128)(2,1)}, u32[]{:S(2)}, u32[]{:S(2)}) %all-to-all-start.1) | async-done | bytes 2621472 | tf_op jit(solution)/shard_map/all_to_all | solution.py:71
  291.6 4.8 %all-to-all-start.3 = ((bf16[16,64,1280]{2,1,0:T(8,128)(2,1)}), bf16[16,64,1280]{2,1,0:T(8,128)(2,1)}, u32[]{:S(2)}, u32[]{:S(2)}) async-start(bf16[16,64,1280]{2,1,0:T(8,128)(2,1)} %bitcast.65), calls=%async_computation.3 | async-start | bytes 5242880 | tf_op jit(solution)/shard_map/all_to_all | solution.py:89
  296.4 5.9 %fusion.1 = bf16[1,1280,768]{2,1,0:T(8,128)(2,1)} fusion(bf16[1024,1280]{1,0:T(8,128)(2,1)} %bitcast.2, bf16[1024,768]{1,0:T(8,128)(2,1)} %all-gather.5.cloned.1.call-done), kind=kOutput, calls=%fused_computation.13 | convolution fusion | flops 2014248960 | bytes 6160384 | tf_op jit(solution)/shard_map/dot_general | solution.py:78
  302.3 5.3 %fusion.2 = bf16[1,768,1280]{2,1,0:T(8,128)(2,1)} fusion(bf16[1024,768]{1,0:T(8,128)(2,1)S(1)} %copy-done.5, bf16[1024,1280]{1,0:T(8,128)(2,1)} %bitcast.8), kind=kOutput, calls=%fused_computation.14 | convolution fusion | flops 2014248960 | bytes 6160384 | tf_op jit(solution)/shard_map/dot_general | solution.py:75
  307.5 7.3 %gather_fusion.1 = bf16[768,1280]{1,0:T(8,128)(2,1)} fusion(bf16[1024,1280]{1,0:T(8,128)(2,1)} %bitcast.6, s32[1024]{0:T(1024)S(1)} %pad_clamp_fusion), kind=kCustom, calls=%fused_computation.1 | custom fusion | bytes 3935232 | tf_op jit(solution)/shard_map/gather | solution.py:93
  314.8 40.3 %all-to-all-done.3 = bf16[16,64,1280]{2,1,0:T(8,128)(2,1)} async-done(((bf16[16,64,1280]{2,1,0:T(8,128)(2,1)}), bf16[16,64,1280]{2,1,0:T(8,128)(2,1)}, u32[]{:S(2)}, u32[]{:S(2)}) %all-to-all-start.3) | async-done | bytes 2621472 | tf_op jit(solution)/shard_map/all_to_all | solution.py:89
  355.2 7.2 %gather_fusion.4 = bf16[768,1280]{1,0:T(8,128)(2,1)} fusion(bf16[1024,1280]{1,0:T(8,128)(2,1)} %bitcast.10, s32[1024]{0:T(1024)S(1)} %pad_clamp_fusion), kind=kCustom, calls=%fused_computation.4 | custom fusion | bytes 3935232 | tf_op jit(solution)/shard_map/gather | solution.py:93
  362.4 4.1 %gather.22 = bf16[128,6,1280]{2,1,0:T(8,128)(2,1)} reshape(bf16[768,1280]{1,0:T(8,128)(2,1)} %gather_fusion.4) | data formatting | bytes 3932160 | tf_op jit(solution)/shard_map/gather | solution.py:93
  370.6 4.5 %reshape.104 = f32[128,6,1280]{2,1,0:T(8,128)} reshape(bf16[768,1280]{1,0:T(8,128)(2,1)} %gather_fusion.1) | data formatting | bytes 5898240 | tf_op jit(solution)/shard_map/convert_element_type | solution.py:93
  375.1 4.9 %multiply_reduce_fusion = bf16[128,1280]{1,0:T(8,128)(2,1)} fusion(f32[128,6,1280]{2,1,0:T(8,128)} %reshape.104, f32[128,6]{1,0:T(8,128)S(1)} %copy-done.2), kind=kLoop, calls=%fused_computation.8 | loop fusion | flops 1802240 | bytes 4262912 | tf_op jit(solution)/shard_map/reduce_sum | solution.py:95
  (51 shorter events, 29.4 us)
Async XLA Ops:
  7.2 92.8 %copy-start = (bf16[1,768,1280]{2,1,0:T(8,128)(2,1)S(1)}, bf16[1,768,1280]{2,1,0:T(8,128)(2,1)}, u32[]{:S(2)}) copy-start(bf16[1,768,1280]{2,1,0:T(8,128)(2,1)} %param.11) | copy-start | bytes 5898244
  10.1 5.7 %copy-start.1 = (f32[128,6]{1,0:T(8,128)}, f32[128,6]{1,0:T(8,128)S(1)}, u32[]{:S(2)}) copy-start(f32[128,6]{1,0:T(8,128)S(1)} %copy.21) | copy-start | bytes 9220
  15.9 4.6 %copy-start.3 = (bf16[128,1280]{1,0:T(8,128)(2,1)S(1)}, bf16[128,1280]{1,0:T(8,128)(2,1)}, u32[]{:S(2)}) copy-start(bf16[128,1280]{1,0:T(8,128)(2,1)} %param.7) | copy-start | bytes 983044
  29.7 6.7 %copy-start.4 = (bf16[128,1280]{1,0:T(8,128)(2,1)S(1)}, bf16[128,1280]{1,0:T(8,128)(2,1)}, u32[]{:S(2)}) copy-start(bf16[128,1280]{1,0:T(8,128)(2,1)} %param.6) | copy-start | bytes 983044
  29.8 65.4 %all-to-all-start.2 = ((bf16[16,64,1280]{2,1,0:T(8,128)(2,1)}), bf16[16,64,1280]{2,1,0:T(8,128)(2,1)}, u32[]{:S(2)}, u32[]{:S(2)}) async-start(bf16[16,64,1280]{2,1,0:T(8,128)(2,1)} %fusion), calls=%async_computation.2 | async-start | bytes 5242880 | tf_op jit(solution)/shard_map/all_to_all | solution.py:72
  95.2 63.5 %all-to-all-start = ((bf16[16,64,1280]{2,1,0:T(8,128)(2,1)}), bf16[16,64,1280]{2,1,0:T(8,128)(2,1)}, u32[]{:S(2)}, u32[]{:S(2)}) async-start(bf16[16,64,1280]{2,1,0:T(8,128)(2,1)} %bitcast.60), calls=%async_computation | async-start | bytes 5242880 | tf_op jit(solution)/shard_map/all_to_all | solution.py:59
  99.9 65.0 %reduce-scatter.9.cloned.1.call-start = ((), (), s32[]{:S(2)}) async-start(), calls=%async_computation.9 | async-start | bytes 2359296
  105.6 84.8 %reduce-scatter.7.cloned.1.call-start = ((), (), s32[]{:S(2)}) async-start(), calls=%async_computation.8 | async-start | bytes 2359296
  164.9 56.3 %all-gather.3.cloned.1.call-start = ((), (), s32[]{:S(2)}) async-start(), calls=%async_computation.6 | async-start | bytes 2359296 | tf_op jit(solution)/shard_map/all_gather | solution.py:18
  226.4 65.3 %all-to-all-start.1 = ((bf16[16,64,1280]{2,1,0:T(8,128)(2,1)}), bf16[16,64,1280]{2,1,0:T(8,128)(2,1)}, u32[]{:S(2)}, u32[]{:S(2)}) async-start(bf16[16,64,1280]{2,1,0:T(8,128)(2,1)} %bitcast.64), calls=%async_computation.1 | async-start | bytes 5242880 | tf_op jit(solution)/shard_map/all_to_all | solution.py:71
  232.9 29.3 %all-gather.5.cloned.1.call-start = ((), (), s32[]{:S(2)}) async-start(), calls=%async_computation.7 | async-start | bytes 2359296 | tf_op jit(solution)/shard_map/all_gather | solution.py:29
  291.6 63.5 %all-to-all-start.3 = ((bf16[16,64,1280]{2,1,0:T(8,128)(2,1)}), bf16[16,64,1280]{2,1,0:T(8,128)(2,1)}, u32[]{:S(2)}, u32[]{:S(2)}) async-start(bf16[16,64,1280]{2,1,0:T(8,128)(2,1)} %bitcast.65), calls=%async_computation.3 | async-start | bytes 5242880 | tf_op jit(solution)/shard_map/all_to_all | solution.py:89
  296.4 5.9 %copy-start.5 = (bf16[1024,768]{1,0:T(8,128)(2,1)S(1)}, bf16[1024,768]{1,0:T(8,128)(2,1)}, u32[]{:S(2)}) copy-start(bf16[1024,768]{1,0:T(8,128)(2,1)} %all-gather.3.cloned.1.call-done) | copy-start | bytes 4718596
  370.6 4.5 %copy-start.2 = (f32[128,6]{1,0:T(8,128)S(1)}, f32[128,6]{1,0:T(8,128)}, u32[]{:S(2)}) copy-start(f32[128,6]{1,0:T(8,128)} %copy-done.1) | copy-start | bytes 9220
Sparse Core Ops, SparseCore 0:
  105.7 26.5 reduce-scatter.8
  165.0 25.3 reduce-scatter.6
  194.0 27.1 all-gather.2
  235.5 26.6 all-gather.4
where the time goes:
time: 387 us; the launch traced here: 386 us
  waiting for transfers between devices  251 us (65%)
  local copies, waits for them, and re-layouts  50.8 us (13%)
  matrix products  30.5 us (8%)
  starting transfers between devices  22.9 us (6%)
  other arithmetic  17.3 us (4%)
  between operations  14 us (4%)
    all_to_all x1, waiting for transfers between devices, local(): lax.all_to_all(send_dy, 'expert', split_axis=0, concat_axis=0, tiled=True)  53.3 us
    all_to_all x1, waiting for transfers between devices, local(): lax.all_to_all(send_x, 'expert', split_axis=0, concat_axis=0, tiled=True)  53 us
    all_to_all x1, waiting for transfers between devices, local(): lax.all_to_all(back_rows, 'expert', split_axis=0, concat_axis=0, tiled=True)  40.3 us
    all_gather x1, waiting for transfers between devices, expert_slope(): return lax.all_gather(share_delta, 'dp', axis=1, tiled=True)  28.8 us
    all_gather x1, waiting for transfers between devices, expert_hidden(): return (share_sum, lax.all_gather(share_act, 'dp', axis=1, tiled=True))  27.4 us
    unnamed x6, waiting for transfers between devices  24.6 us
    all_to_all x1, waiting for transfers between devices, local(): lax.all_to_all(out_rows, 'expert', split_axis=0, concat_axis=0, tiled=True)  23.6 us
    gather x3, local copies, waits for them, and re-layouts, gather_rows(): flat_rows[slot_index].astype(jnp.float32)  18.6 us
  transfers between devices with their start and end apart: 8, of which 7 were waited for; matrix products, arithmetic and copies ran while one was open for 11% of the time, Pallas kernels for 0%

commit v1 on v0

--- a/solution.py
+++ b/solution.py
@@ -1,6 +1,10 @@
+import functools
+
 import jax
 import jax.numpy as jnp
 from jax import lax
+from jax.experimental import pallas as pl
+from jax.experimental.pallas import tpu as pltpu
 from jax.sharding import PartitionSpec as P
 
 
@@ -29,7 +33,7 @@
     return lax.all_gather(share_delta, "dp", axis=1, tiled=True)
 
 
-def local(tokens, cotangent, expert_ids, gate_weights, w_in, w_out):
+def local_slots(tokens, cotangent, expert_ids, gate_weights, w_in, w_out):
     experts = lax.axis_size("expert")
     tok_rows, quarter = tokens.shape
     choose_count = expert_ids.shape[1]
@@ -99,6 +103,385 @@
     return (mixed_out, token_grad, in_grad, out_grad)
 
 
+BF16, F32 = jnp.bfloat16, jnp.float32
+MESH = pl.DeviceIdType.MESH
+
+
+def mm(a, b, dims=((1,), (0,))):
+    return lax.dot_general(a, b, (dims, ((), ())), preferred_element_type=F32)
+
+
+def fused_kernel(
+    n, cap,
+    x_ref, dy_ref, meta_ref, win_ref, wout_ref,
+    mixed_ref, tgrad_ref, ingrad_ref, outgrad_ref,
+    xg, dyg, mg, rows_x, rows_dy, sel, selcat, gate, hp_s, hp_r, sp_s, sp_r, act, delta,
+    ocat, osnd, bcat, bsnd, rso_s, rso_r, rsb_s, rsb_r,
+    ring_s, ring_r, sib_s, sib_r, mring_s, mring_r, msib_s, msib_r,
+    hx_s, hx_r, cx_s, cx_r, rs_s, rs_r,
+):
+    half = n // 2
+    me = lax.axis_index("expert")
+    dp_me = lax.axis_index("dp")
+    core = me % 2
+    chip = me // 2
+    odd = chip % 2
+    pos = (chip // 2) * (1 - 2 * odd) + odd * (n - 1)
+
+    def device_at(p):
+        hi = p // half
+        return ((1 - hi) * 2 * p + hi * (2 * n - 1 - 2 * p)) * 2 + core
+
+    right = {"expert": device_at((pos + 1) % n)}
+    left = {"expert": device_at((pos + n - 1) % n)}
+    sib = {"expert": me + 1 - 2 * core}
+    peer = {"dp": 1 - dp_me}
+    ring_to = (right, left)
+
+    barrier = pltpu.get_barrier_semaphore()
+    for d in (right, left, sib, peer):
+        pl.semaphore_signal(barrier, inc=1, device_id=d, device_id_type=MESH)
+    pl.semaphore_wait(barrier, 4)
+
+    tok = x_ref.shape[0]
+    hrow = tok // 2
+
+    def rcopy(src, dst, ssem, rsem, dev):
+        return pltpu.make_async_remote_copy(
+            src_ref=src, dst_ref=dst, send_sem=ssem, recv_sem=rsem,
+            device_id=dev, device_id_type=MESH,
+        )
+
+    pending = []
+
+    def off(d, h):
+        return (-h if d == 0 else h) % n
+
+    def chunks_at(d, h):
+        return (0, 1) if h < half else (d,)
+
+    def ring_copy(t, d, h, c):
+        own, buf = ((x_ref, xg), (dy_ref, dyg))[t]
+        rows = pl.ds(c * hrow, hrow)
+        src = own.at[rows] if h == 1 else buf.at[off(d, h - 1), 0, rows]
+        return rcopy(src, buf.at[off(d, h), 0, rows], ring_s.at[t, d, h - 1, c], ring_r.at[t, d, h - 1, c], ring_to[d])
+
+    def sib_copy(t, o):
+        own, buf = ((x_ref, xg), (dy_ref, dyg))[t]
+        src = own if o == 0 else buf.at[o, 0]
+        return rcopy(src, buf.at[o, 1], sib_s.at[t, o], sib_r.at[t, o], sib)
+
+    def meta_ring(d, h):
+        src = meta_ref if h == 1 else mg.at[off(d, h - 1), 0]
+        return rcopy(src, mg.at[off(d, h), 0], mring_s.at[d, h - 1], mring_r.at[d, h - 1], ring_to[d])
+
+    def meta_sib(o):
+        src = meta_ref if o == 0 else mg.at[o, 0]
+        return rcopy(src, mg.at[o, 1], msib_s.at[o], msib_r.at[o], sib)
+
+    def go(copy):
+        copy.start()
+        pending.append(copy)
+
+    def send_first(t):
+        if t == 0:
+            for d in (0, 1):
+                go(meta_ring(d, 1))
+            go(meta_sib(0))
+        for c in (0, 1):
+            for d in (0, 1):
+                go(ring_copy(t, d, 1, c))
+        go(sib_copy(t, 0))
+
+    def hop(t, h):
+        if t == 0:
+            for d in (0, 1):
+                if h < half or d == 0:
+                    meta_ring(d, h).wait_recv()
+                    if h + 1 < half or (h + 1 == half and d == 0):
+                        go(meta_ring(d, h + 1))
+                    go(meta_sib(off(d, h)))
+        for c in (0, 1):
+            for d in (0, 1):
+                if c in chunks_at(d, h):
+                    ring_copy(t, d, h, c).wait_recv()
+                    if h < half and c in chunks_at(d, h + 1):
+                        go(ring_copy(t, d, h + 1, c))
+        if h < half:
+            for d in (0, 1):
+                go(sib_copy(t, off(d, h)))
+        else:
+            go(sib_copy(t, half))
+
+    before = (
+        lax.broadcasted_iota(jnp.int32, (tok, tok), 0) < lax.broadcasted_iota(jnp.int32, (tok, tok), 1)
+    ).astype(F32).astype(BF16)
+    slot = lax.broadcasted_iota(jnp.int32, (cap, tok), 0).astype(F32)
+
+    def routing(meta, expert):
+        hit = (meta[0:8] == expert).astype(F32)
+        g = jnp.sum(hit * meta[8:16], axis=0, keepdims=True)
+        named = jnp.sum(hit, axis=0, keepdims=True)
+        earlier = mm(jnp.broadcast_to(named, (8, tok)).astype(BF16), before)[0:1]
+        chosen = jnp.where(earlier == slot, named, 0.0)
+        return chosen.astype(BF16), jnp.sum(chosen * g, axis=1, keepdims=True)
+
+    me_f = me.astype(F32)
+    sib_f = (me + 1 - 2 * core).astype(F32)
+
+    def span(o):
+        return pl.ds(o * 2 * cap, 2 * cap)
+
+    def take_x(o):
+        sib_copy(0, o).wait_recv()
+        meta_sib(o).wait_recv()
+        for s in (0, 1):
+            first = o == 0 and s == 0
+            meta = meta_ref[...] if first else mg[o, s]
+            block = x_ref[...] if first else xg[o, s]
+            chosen, g = routing(meta, me_f)
+            rows = pl.ds(o * 2 * cap + s * cap, cap)
+            sel[rows] = chosen
+            gate[rows] = g
+            rows_x[rows] = mm(chosen, block).astype(BF16)
+            if s == 0:
+                selcat[pl.ds(o * 2 * cap, cap)] = chosen
+                selcat[pl.ds(o * 2 * cap + cap, cap)] = routing(meta, sib_f)[0]
+        hp_s[span(o)] = mm(rows_x[span(o)], win_ref[...]).astype(BF16)
+        go(dp_copy(0, o))
+
+    def dp_copy(t, o):
+        s_buf, r_buf = ((hp_s, hp_r), (sp_s, sp_r))[t]
+        return rcopy(s_buf.at[span(o)], r_buf.at[span(o)], hx_s.at[t, o], hx_r.at[t, o], peer)
+
+    def take_dy(o):
+        sib_copy(1, o).wait_recv()
+        for s in (0, 1):
+            rows = pl.ds(o * 2 * cap + s * cap, cap)
+            block = dy_ref[...] if (o == 0 and s == 0) else dyg[o, s]
+            rows_dy[rows] = (gate[rows] * mm(sel[rows], block)).astype(BF16)
+        sp_s[span(o)] = mm(rows_dy[span(o)], wout_ref[...], ((1,), (1,))).astype(BF16)
+        go(dp_copy(1, o))
+
+    def cat_copy(t, o):
+        s_buf, r_buf = ((osnd, ocat), (bsnd, bcat))[t]
+        return rcopy(
+            s_buf.at[pl.ds(o * cap, cap)], r_buf.at[pl.ds(o * 2 * cap + cap, cap)],
+            cx_s.at[t, o], cx_r.at[t, o], sib,
+        )
+
+    def hidden_of(o):
+        return hp_s[span(o)].astype(F32) + hp_r[span(o)].astype(F32)
+
+    def give(t, o, rows):
+        s_buf, r_buf = ((osnd, ocat), (bsnd, bcat))[t]
+        r_buf[pl.ds(o * 2 * cap, cap)] = rows[:cap]
+        s_buf[pl.ds(o * cap, cap)] = rows[cap:]
+        go(cat_copy(t, o))
+
+    def forward(o):
+        dp_copy(0, o).wait_recv()
+        activation = jax.nn.silu(hidden_of(o)).astype(BF16)
+        act[span(o)] = activation
+        out_rows = mm(activation, wout_ref[...]).astype(BF16)
+        give(0, o, (gate[span(o)] * out_rows.astype(F32)).astype(BF16))
+
+    def backward(o):
+        dp_copy(1, o).wait_recv()
+        slope = sp_s[span(o)].astype(F32) + sp_r[span(o)].astype(F32)
+        d_hidden = (slope * silu_slope(hidden_of(o))).astype(BF16)
+        delta[span(o)] = d_hidden
+        give(1, o, mm(d_hidden, win_ref[...], ((1,), (1,))).astype(BF16))
+
+    def contribution(t, o, c):
+        buf = (ocat, bcat)[t]
+        return mm(selcat[span(o), c * hrow:(c + 1) * hrow], buf[span(o)], ((0,), (0,)))
+
+    def rs_copy(t, d, h, c):
+        s_buf, r_buf = ((rso_s, rso_r), (rsb_s, rsb_r))[t]
+        rows = pl.ds(c * hrow, hrow)
+        return rcopy(
+            s_buf.at[d, h - 1, rows], r_buf.at[d, h - 1, rows],
+            rs_s.at[t, d, h - 1, c], rs_r.at[t, d, h - 1, c], ring_to[d],
+        )
+
+    def rs_hop(t, h):
+        s_buf, r_buf = ((rso_s, rso_r), (rsb_s, rsb_r))[t]
+        for o in {off(1, h), off(0, h)}:
+            cat_copy(t, o).wait_recv()
+        for c in (0, 1):
+            for d in (0, 1):
+                if c not in chunks_at(d, h):
+                    continue
+                rows = pl.ds(c * hrow, hrow)
+                total = contribution(t, off(1 - d, h), c)
+                if h < half and c in chunks_at(d, h + 1):
+                    rs_copy(t, d, h + 1, c).wait_recv()
+                    total = total + r_buf[d, h, rows].astype(F32)
+                s_buf[d, h - 1, rows] = total.astype(BF16)
+                go(rs_copy(t, d, h, c))
+
+    def rs_last(t):
+        r_buf = (rso_r, rsb_r)[t]
+        out = (mixed_ref, tgrad_ref)[t]
+        cat_copy(t, 0).wait_recv()
+        for c in (0, 1):
+            rows = pl.ds(c * hrow, hrow)
+            total = contribution(t, 0, c)
+            for d in (0, 1):
+                rs_copy(t, d, 1, c).wait_recv()
+                total = total + r_buf[d, 0, rows].astype(F32)
+            out[rows] = total.astype(BF16)
+
+    def out_grad():
+        f_hidden = act.shape[1]
+        tile = 256 if f_hidden % 256 == 0 else f_hidden
+
+        @pl.loop(0, f_hidden // tile)
+        def _(i):
+            cols = pl.ds(pl.multiple_of(i * tile, tile), tile)
+            outgrad_ref[cols] = mm(act[:, cols], rows_dy[...], ((0,), (0,))).astype(BF16)
+
+    def in_grad():
+        width = rows_x.shape[1]
+        tile = 256 if width % 256 == 0 else width
+
+        @pl.loop(0, width // tile)
+        def _(i):
+            cols = pl.ds(pl.multiple_of(i * tile, tile), tile)
+            ingrad_ref[cols] = mm(rows_x[:, cols], delta[...], ((0,), (0,))).astype(BF16)
+
+    order = [[0]] + [[off(0, h), off(1, h)] for h in range(1, half)] + [[half]]
+    send_first(0)
+    for h in range(1, half):
+        hop(0, h)
+        for o in order[h - 1]:
+            take_x(o)
+    send_first(1)
+    hop(0, half)
+    for o in order[half - 1]:
+        take_x(o)
+    hop(1, 1)
+    take_x(half)
+    for h in range(2, half):
+        hop(1, h)
+        for o in order[h - 2]:
+            take_dy(o)
+            forward(o)
+    hop(1, half)
+    for i in (half - 2, half - 1, half):
+        for o in order[i]:
+            take_dy(o)
+    for i in (half, half - 1, half - 2):
+        for o in order[i]:
+            forward(o)
+    for h in range(half, 0, -1):
+        rs_hop(0, h)
+        for o in order[half - h]:
+            backward(o)
+    for o in order[half]:
+        backward(o)
+    rs_hop(1, half)
+    rs_last(0)
+    for h in range(half - 1, 0, -1):
+        rs_hop(1, h)
+        if h == half - 1:
+            out_grad()
+        if h == half - 2:
+            in_grad()
+    rs_last(1)
+    for copy in pending:
+        copy.wait_send()
+
+
+def local_fused(tokens, cotangent, expert_ids, gate_weights, w_in, w_out):
+    experts = lax.axis_size("expert")
+    tok_rows, width = tokens.shape
+    top = expert_ids.shape[1]
+    hid = w_in.shape[2]
+    cap = max(2, 4 * tok_rows * top // (3 * experts))
+    n = experts // 2
+    half = n // 2
+    slots = experts * cap
+    pad = 8 - top
+    meta = jnp.concatenate(
+        [
+            jnp.pad(expert_ids.T.astype(F32), ((0, pad), (0, 0)), constant_values=-1.0),
+            jnp.pad(gate_weights.T, ((0, pad), (0, 0))),
+        ],
+        0,
+    )
+    vm = pltpu.VMEM
+    dma = pltpu.SemaphoreType.DMA
+    mixed, tgrad, ingrad, outgrad = pl.pallas_call(
+        functools.partial(fused_kernel, n, cap),
+        out_shape=(
+            jax.ShapeDtypeStruct((tok_rows, width), BF16),
+            jax.ShapeDtypeStruct((tok_rows, width), BF16),
+            jax.ShapeDtypeStruct((width, hid), BF16),
+            jax.ShapeDtypeStruct((hid, width), BF16),
+        ),
+        in_specs=[pl.BlockSpec(memory_space=pltpu.VMEM)] * 5,
+        out_specs=[pl.BlockSpec(memory_space=pltpu.VMEM)] * 4,
+        scratch_shapes=[
+            vm((n, 2, tok_rows, width), BF16),
+            vm((n, 2, tok_rows, width), BF16),
+            vm((n, 2, 16, tok_rows), F32),
+            vm((slots, width), BF16),
+            vm((slots, width), BF16),
+            vm((slots, tok_rows), BF16),
+            vm((slots, tok_rows), BF16),
+            vm((slots, 1), F32),
+            vm((slots, hid), BF16),
+            vm((slots, hid), BF16),
+            vm((slots, hid), BF16),
+            vm((slots, hid), BF16),
+            vm((slots, hid), BF16),
+            vm((slots, hid), BF16),
+            vm((slots, width), BF16),
+            vm((slots // 2, width), BF16),
+            vm((slots, width), BF16),
+            vm((slots // 2, width), BF16),
+            vm((2, half, tok_rows, width), BF16),
+            vm((2, half, tok_rows, width), BF16),
+            vm((2, half, tok_rows, width), BF16),
+            vm((2, half, tok_rows, width), BF16),
+            dma((2, 2, half, 2)),
+            dma((2, 2, half, 2)),
+            dma((2, n)),
+            dma((2, n)),
+            dma((2, half)),
+            dma((2, half)),
+            dma((n,)),
+            dma((n,)),
+            dma((2, n)),
+            dma((2, n)),
+            dma((2, n)),
+            dma((2, n)),
+            dma((2, 2, half, 2)),
+            dma((2, 2, half, 2)),
+        ],
+        compiler_params=pltpu.CompilerParams(
+            collective_id=0, has_side_effects=True, vmem_limit_bytes=67043328
+        ),
+        name="fused_experts",
+    )(tokens, cotangent, meta, w_in[0], w_out[0])
+    return (mixed, tgrad, ingrad[None], outgrad[None])
+
+
+def gathers_pay(mesh, tok_rows, top):
+    experts = mesh.shape["expert"]
+    cap = max(2, 4 * tok_rows * top // (3 * experts))
+    return (
+        mesh.shape["dp"] == 2
+        and experts % 8 == 0
+        and top <= 8
+        and tok_rows % 128 == 0
+        and cap % 16 == 0
+        and tok_rows <= 2 * cap
+    )
+
+
 def solution(mesh):
     in_specs = (
         P("expert", "dp"),
@@ -114,4 +497,14 @@
         P("expert", "dp", None),
         P("expert", None, "dp"),
     )
-    return jax.shard_map(local, mesh=mesh, in_specs=in_specs, out_specs=out_specs, check_vma=False)
+
+    def run(tokens, cotangent, expert_ids, gate_weights, w_in, w_out):
+        rows, top = expert_ids.shape
+        fused = gathers_pay(mesh, rows // mesh.shape["expert"], top)
+        body = jax.shard_map(
+            local_fused if fused else local_slots,
+            mesh=mesh, in_specs=in_specs, out_specs=out_specs, check_vma=False,
+        )
+        return body(tokens, cotangent, expert_ids, gate_weights, w_in, w_out)
+
+    return run

time: 387 us -> 139 us (0.36)
  waiting for transfers between devices: 251 us -> 0 us
  Pallas kernels: 0 us -> 126 us
  local copies, waits for them, and re-layouts: 50.8 us -> 7.79 us
  matrix products: 30.5 us -> 0 us
  starting transfers between devices: 22.9 us -> 0 us
  other arithmetic: 17.3 us -> 1.98 us
  between operations: 14 us -> 0.64 us
    all_to_all x4 -> x0, waiting for transfers between devices: 170 us -> none  [the longest x1 53.3 us: local(): lax.all_to_all(send_dy, 'expert', split_axis=0, concat_axis=0, tiled=True)]
    pallas_call x0 -> x1, Pallas kernels: none -> 126 us  [local_fused(): pl.pallas_call(functools.partial(fused_kernel, n, cap), out_shape=(jax.Sh...]
    all_gather x2 -> x0, waiting for transfers between devices: 56.1 us -> none  [the longest x1 28.8 us: expert_slope(): return lax.all_gather(share_delta, 'dp', axis=1, tiled=True)]
    gather x6 -> x0, local copies, waits for them, and re-layouts: 34.1 us -> none  [the longest x3 18.6 us: gather_rows(): flat_rows[slot_index].astype(jnp.float32)]
    dot_general x6 -> x0, matrix products: 30.5 us -> none  [the longest x1 5.85 us: local(): lax.dot_general(rows_x, delta_hidden, (((0,), (0,)), ((), ())), preferred...]
    unnamed x6 -> x0, waiting for transfers between devices: 24.6 us -> none
    all_to_all x4 -> x0, starting transfers between devices: 22.7 us -> none  [the longest x1 6.65 us: local(): lax.all_to_all(send_dy, 'expert', split_axis=0, concat_axis=0, tiled=True)]
    reduce_sum x3 -> x0, other arithmetic: 9.03 us -> none  [the longest x1 4.87 us: local(): jnp.sum(gather_rows(returned_out) * gate_weights[:, :, None], axis=1)]
  transfers between devices with their start and end apart: 8 -> 0, of which waited for: 7 -> 0; matrix products, arithmetic and copies ran while one was open for 11% -> 0% of each run, Pallas kernels for 0% -> 0%
where the time goes in v1:
time: 139 us; the launch traced here: 136 us
  Pallas kernels  126 us (91%)
  local copies, waits for them, and re-layouts  7.79 us (6%)
  other arithmetic  1.98 us (1%)
    pallas_call x1, Pallas kernels, local_fused(): pl.pallas_call(functools.partial(fused_kernel, n, cap), out_shape=(jax.Sh...  126 us
    unnamed x6, local copies, waits for them, and re-layouts  7.79 us

profile of v1, /device:TPU:13, one launch (start us, length us, event | category | flops | bytes accessed | tf_op | source)
XLA Modules:
  0.0 136.4 jit_solution(7845441346543002833)
XLA Ops:
  0.6 0.7 convert_bitcast_fusion
  1.3 1.3 select_maximum_fusion.meta_ref
  2.6 126.0 %fused_experts.1 = (bf16[128,1280]{1,0:T(8,128)(2,1)}, bf16[128,1280]{1,0:T(8,128)(2,1)}, bf16[1280,768]{1,0:T(8,128)(2,1)}, bf16[768,1280]{1,0:T(8,128)(2,1)}) custom-call(bf16[128,1280]{1,0:T(8,128)(2,1)} %x_ref.1, bf16[128,1280]{1,0:T(8,128)(2,1)} %dy_ref.1, f32[16,128]{1,0:T(8,128)} %select_maximum_fusion.meta_ref, bf16[1280,768]{1,0:T(8,128)(2,1)} %bitcast.7, ...), custom_call_target="tpu_custom_call" | custom-call | tf_op jit(solution)/shard_map/fused_experts/pallas_call | solution.py:416
  128.6 1.7 %copy.14 = bf16[128,1280]{1,0:T(8,128)(2,1)} copy(bf16[128,1280]{1,0:T(8,128)(2,1)} %get-tuple-element.16) | data formatting | bytes 655360
  130.3 1.7 %copy.15 = bf16[128,1280]{1,0:T(8,128)(2,1)} copy(bf16[128,1280]{1,0:T(8,128)(2,1)} %get-tuple-element.17) | data formatting | bytes 655360
  132.0 0.0 copy-start
  132.0 3.1 %copy.16 = bf16[1,1280,768]{2,1,0:T(8,128)(2,1)} copy(bf16[1,1280,768]{2,1,0:T(8,128)(2,1)} %bitcast.10) | data formatting | bytes 3932160
  135.1 0.0 copy-done
  135.1 1.3 copy.17
Async XLA Ops:
  132.0 3.1 %copy-start = (bf16[768,1280]{1,0:T(8,128)(2,1)S(1)}, bf16[768,1280]{1,0:T(8,128)(2,1)}, u32[]{:S(2)}) copy-start(bf16[768,1280]{1,0:T(8,128)(2,1)} %get-tuple-element.11) | copy-start | bytes 5898244

commit v2 on v1

--- a/solution.py
+++ b/solution.py
@@ -113,12 +113,13 @@
 
 def fused_kernel(
     n, cap,
-    x_ref, dy_ref, meta_ref, win_ref, wout_ref,
-    mixed_ref, tgrad_ref, ingrad_ref, outgrad_ref,
+    x_ref, dy_ref, ids_ref, gates_ref, win_hbm, wout_hbm,
+    mixed_ref, tgrad_ref, ingrad_hbm, outgrad_hbm,
+    win_ref, wout_ref, ingrad_ref, outgrad_ref, meta_ref,
     xg, dyg, mg, rows_x, rows_dy, sel, selcat, gate, hp_s, hp_r, sp_s, sp_r, act, delta,
     ocat, osnd, bcat, bsnd, rso_s, rso_r, rsb_s, rsb_r,
     ring_s, ring_r, sib_s, sib_r, mring_s, mring_r, msib_s, msib_r,
-    hx_s, hx_r, cx_s, cx_r, rs_s, rs_r,
+    hx_s, hx_r, cx_s, cx_r, rs_s, rs_r, load_sem, ig_sem, og_sem,
 ):
     half = n // 2
     me = lax.axis_index("expert")
@@ -138,6 +139,11 @@
     peer = {"dp": 1 - dp_me}
     ring_to = (right, left)
 
+    load_in = pltpu.make_async_copy(win_hbm, win_ref, load_sem.at[0])
+    load_out = pltpu.make_async_copy(wout_hbm, wout_ref, load_sem.at[1])
+    load_in.start()
+    load_out.start()
+
     barrier = pltpu.get_barrier_semaphore()
     for d in (right, left, sib, peer):
         pl.semaphore_signal(barrier, inc=1, device_id=d, device_id_type=MESH)
@@ -166,10 +172,11 @@
         src = own.at[rows] if h == 1 else buf.at[off(d, h - 1), 0, rows]
         return rcopy(src, buf.at[off(d, h), 0, rows], ring_s.at[t, d, h - 1, c], ring_r.at[t, d, h - 1, c], ring_to[d])
 
-    def sib_copy(t, o):
+    def sib_copy(t, o, c):
         own, buf = ((x_ref, xg), (dy_ref, dyg))[t]
-        src = own if o == 0 else buf.at[o, 0]
-        return rcopy(src, buf.at[o, 1], sib_s.at[t, o], sib_r.at[t, o], sib)
+        rows = pl.ds(c * hrow, hrow)
+        src = own.at[rows] if o == 0 else buf.at[o, 0, rows]
+        return rcopy(src, buf.at[o, 1, rows], sib_s.at[t, o, c], sib_r.at[t, o, c], sib)
 
     def meta_ring(d, h):
         src = meta_ref if h == 1 else mg.at[off(d, h - 1), 0]
@@ -184,14 +191,20 @@
         pending.append(copy)
 
     def send_first(t):
-        if t == 0:
-            for d in (0, 1):
-                go(meta_ring(d, 1))
-            go(meta_sib(0))
         for c in (0, 1):
             for d in (0, 1):
                 go(ring_copy(t, d, 1, c))
-        go(sib_copy(t, 0))
+        for c in (0, 1):
+            go(sib_copy(t, 0, c))
+
+    def send_meta():
+        top = ids_ref.shape[0]
+        meta_ref[...] = jnp.full(meta_ref.shape, -1.0, F32)
+        meta_ref[0:top] = ids_ref[...].astype(F32)
+        meta_ref[8:8 + top] = gates_ref[...]
+        for d in (0, 1):
+            go(meta_ring(d, 1))
+        go(meta_sib(0))
 
     def hop(t, h):
         if t == 0:
@@ -207,11 +220,11 @@
                     ring_copy(t, d, h, c).wait_recv()
                     if h < half and c in chunks_at(d, h + 1):
                         go(ring_copy(t, d, h + 1, c))
-        if h < half:
-            for d in (0, 1):
-                go(sib_copy(t, off(d, h)))
-        else:
-            go(sib_copy(t, half))
+                    go(sib_copy(t, off(d, h), c))
+
+    def sib_arrived(t, o):
+        for c in (0, 1):
+            sib_copy(t, o, c).wait_recv()
 
     before = (
         lax.broadcasted_iota(jnp.int32, (tok, tok), 0) < lax.broadcasted_iota(jnp.int32, (tok, tok), 1)
@@ -233,7 +246,7 @@
         return pl.ds(o * 2 * cap, 2 * cap)
 
     def take_x(o):
-        sib_copy(0, o).wait_recv()
+        sib_arrived(0, o)
         meta_sib(o).wait_recv()
         for s in (0, 1):
             first = o == 0 and s == 0
@@ -255,7 +268,7 @@
         return rcopy(s_buf.at[span(o)], r_buf.at[span(o)], hx_s.at[t, o], hx_r.at[t, o], peer)
 
     def take_dy(o):
-        sib_copy(1, o).wait_recv()
+        sib_arrived(1, o)
         for s in (0, 1):
             rows = pl.ds(o * 2 * cap + s * cap, cap)
             block = dy_ref[...] if (o == 0 and s == 0) else dyg[o, s]
@@ -309,8 +322,9 @@
         s_buf, r_buf = ((rso_s, rso_r), (rsb_s, rsb_r))[t]
         for o in {off(1, h), off(0, h)}:
             cat_copy(t, o).wait_recv()
-        for c in (0, 1):
+        for late in (0, 1):
             for d in (0, 1):
+                c = d if late else 1 - d
                 if c not in chunks_at(d, h):
                     continue
                 rows = pl.ds(c * hrow, hrow)
@@ -333,65 +347,111 @@
                 total = total + r_buf[d, 0, rows].astype(F32)
             out[rows] = total.astype(BF16)
 
-    def out_grad():
-        f_hidden = act.shape[1]
-        tile = 256 if f_hidden % 256 == 0 else f_hidden
-
-        @pl.loop(0, f_hidden // tile)
-        def _(i):
-            cols = pl.ds(pl.multiple_of(i * tile, tile), tile)
-            outgrad_ref[cols] = mm(act[:, cols], rows_dy[...], ((0,), (0,))).astype(BF16)
-
-    def in_grad():
-        width = rows_x.shape[1]
-        tile = 256 if width % 256 == 0 else width
-
-        @pl.loop(0, width // tile)
-        def _(i):
-            cols = pl.ds(pl.multiple_of(i * tile, tile), tile)
-            ingrad_ref[cols] = mm(rows_x[:, cols], delta[...], ((0,), (0,))).astype(BF16)
+    def grad_tile(i, left, right, v_ref, hbm, sem):
+        cols = slice(i * tile, (i + 1) * tile)
+        v_ref[cols] = mm(left[:, cols], right[...], ((0,), (0,))).astype(BF16)
+        copy = pltpu.make_async_copy(v_ref.at[cols], hbm.at[cols], sem.at[i])
+        copy.start()
+        stores.append(copy)
+
+    def out_tiles(tiles):
+        for i in tiles:
+            grad_tile(i, act, rows_dy, outgrad_ref, outgrad_hbm, og_sem)
+
+    def in_tiles(tiles):
+        for i in tiles:
+            grad_tile(i, rows_x, delta, ingrad_ref, ingrad_hbm, ig_sem)
+
+    stores = []
+    tile = 256
+    n_out, n_in = act.shape[1] // tile, rows_x.shape[1] // tile
+
+    def part(count, h):
+        k = half - 1 - h
+        return range(count * k // (half - 1), count * (k + 1) // (half - 1))
 
     order = [[0]] + [[off(0, h), off(1, h)] for h in range(1, half)] + [[half]]
+
+    def each(f, i):
+        for o in order[i]:
+            f(o)
+
     send_first(0)
+    send_meta()
+    load_in.wait()
+    take_x(0)
     for h in range(1, half):
         hop(0, h)
-        for o in order[h - 1]:
-            take_x(o)
-    send_first(1)
+        if h == half - 1:
+            send_first(1)
+            load_out.wait()
+        each(take_x, h)
     hop(0, half)
-    for o in order[half - 1]:
-        take_x(o)
-    hop(1, 1)
     take_x(half)
-    for h in range(2, half):
+    for h in range(1, half - 1):
         hop(1, h)
-        for o in order[h - 2]:
-            take_dy(o)
-            forward(o)
+        each(take_dy, h - 1)
+        each(forward, h - 1)
+    hop(1, half - 1)
+    each(take_dy, half - 2)
+    each(forward, half - 2)
+    each(forward, half)
+    each(forward, half - 1)
+    rs_hop(0, half)
     hop(1, half)
-    for i in (half - 2, half - 1, half):
-        for o in order[i]:
-            take_dy(o)
-    for i in (half, half - 1, half - 2):
-        for o in order[i]:
-            forward(o)
-    for h in range(half, 0, -1):
+    each(take_dy, half - 1)
+    rs_hop(0, half - 1)
+    each(take_dy, half)
+    each(backward, 0)
+    out_tiles(part(n_out, half - 1))
+    for h in range(half - 2, 0, -1):
         rs_hop(0, h)
-        for o in order[half - h]:
-            backward(o)
-    for o in order[half]:
-        backward(o)
+        each(backward, half - 1 - h)
+        out_tiles(part(n_out, h))
+    each(backward, half - 1)
+    each(backward, half)
     rs_hop(1, half)
     rs_last(0)
     for h in range(half - 1, 0, -1):
         rs_hop(1, h)
-        if h == half - 1:
-            out_grad()
-        if h == half - 2:
-            in_grad()
+        in_tiles(part(n_in, h))
     rs_last(1)
+    for copy in stores:
+        copy.wait()
     for copy in pending:
         copy.wait_send()
+
+
+def copy_kernel(count, *refs):
+    srcs, dsts, bufs = refs[:count], refs[count:2 * count], refs[2 * count:3 * count]
+    in_sem, out_sem = refs[3 * count:]
+    into, outof = [], []
+    for j in range(count):
+        rows = srcs[j].shape[0] // 4
+        for q in range(4):
+            at = pl.ds(q * rows, rows)
+            into.append(pltpu.make_async_copy(srcs[j].at[at], bufs[j].at[at], in_sem.at[j, q]))
+            outof.append(pltpu.make_async_copy(bufs[j].at[at], dsts[j].at[at], out_sem.at[j, q]))
+    for copy in into:
+        copy.start()
+    for a, b in zip(into, outof):
+        a.wait()
+        b.start()
+    for copy in outof:
+        copy.wait()
+
+
+def settle(arrays):
+    count = len(arrays)
+    return pl.pallas_call(
+        functools.partial(copy_kernel, count),
+        out_shape=[jax.ShapeDtypeStruct(a.shape, a.dtype) for a in arrays],
+        in_specs=[pl.BlockSpec(memory_space=pl.ANY)] * count,
+        out_specs=[pl.BlockSpec(memory_space=pl.ANY)] * count,
+        scratch_shapes=[pltpu.VMEM(a.shape, a.dtype) for a in arrays]
+        + [pltpu.SemaphoreType.DMA((count, 4))] * 2,
+        name="settle",
+    )(*arrays)
 
 
 def local_fused(tokens, cotangent, expert_ids, gate_weights, w_in, w_out):
@@ -403,14 +463,6 @@
     n = experts // 2
     half = n // 2
     slots = experts * cap
-    pad = 8 - top
-    meta = jnp.concatenate(
-        [
-            jnp.pad(expert_ids.T.astype(F32), ((0, pad), (0, 0)), constant_values=-1.0),
-            jnp.pad(gate_weights.T, ((0, pad), (0, 0))),
-        ],
-        0,
-    )
     vm = pltpu.VMEM
     dma = pltpu.SemaphoreType.DMA
     mixed, tgrad, ingrad, outgrad = pl.pallas_call(
@@ -421,9 +473,14 @@
             jax.ShapeDtypeStruct((width, hid), BF16),
             jax.ShapeDtypeStruct((hid, width), BF16),
         ),
-        in_specs=[pl.BlockSpec(memory_space=pltpu.VMEM)] * 5,
-        out_specs=[pl.BlockSpec(memory_space=pltpu.VMEM)] * 4,
+        in_specs=[pl.BlockSpec(memory_space=pltpu.VMEM)] * 4 + [pl.BlockSpec(memory_space=pl.ANY)] * 2,
+        out_specs=[pl.BlockSpec(memory_space=pltpu.VMEM)] * 2 + [pl.BlockSpec(memory_space=pl.ANY)] * 2,
         scratch_shapes=[
+            vm((width, hid), BF16),
+            vm((hid, width), BF16),
+            vm((width, hid), BF16),
+            vm((hid, width), BF16),
+            vm((16, tok_rows), F32),
             vm((n, 2, tok_rows, width), BF16),
             vm((n, 2, tok_rows, width), BF16),
             vm((n, 2, 16, tok_rows), F32),
@@ -448,8 +505,8 @@
             vm((2, half, tok_rows, width), BF16),
             dma((2, 2, half, 2)),
             dma((2, 2, half, 2)),
-            dma((2, n)),
-            dma((2, n)),
+            dma((2, n, 2)),
+            dma((2, n, 2)),
             dma((2, half)),
             dma((2, half)),
             dma((n,)),
@@ -460,16 +517,20 @@
             dma((2, n)),
             dma((2, 2, half, 2)),
             dma((2, 2, half, 2)),
+            dma((2,)),
+            dma((width // 256,)),
+            dma((hid // 256,)),
         ],
         compiler_params=pltpu.CompilerParams(
             collective_id=0, has_side_effects=True, vmem_limit_bytes=67043328
         ),
         name="fused_experts",
-    )(tokens, cotangent, meta, w_in[0], w_out[0])
+    )(tokens, cotangent, expert_ids.T, gate_weights.T, w_in[0], w_out[0])
+    mixed, tgrad, ingrad, outgrad = settle([mixed, tgrad, ingrad, outgrad])
     return (mixed, tgrad, ingrad[None], outgrad[None])
 
 
-def gathers_pay(mesh, tok_rows, top):
+def gathers_pay(mesh, tok_rows, top, width, hid):
     experts = mesh.shape["expert"]
     cap = max(2, 4 * tok_rows * top // (3 * experts))
     return (
@@ -479,6 +540,8 @@
         and tok_rows % 128 == 0
         and cap % 16 == 0
         and tok_rows <= 2 * cap
+        and width % 256 == 0
+        and hid % 256 == 0
     )
 
 
@@ -500,7 +563,8 @@
 
     def run(tokens, cotangent, expert_ids, gate_weights, w_in, w_out):
         rows, top = expert_ids.shape
-        fused = gathers_pay(mesh, rows // mesh.shape["expert"], top)
+        width = tokens.shape[1] // mesh.shape["dp"]
+        fused = gathers_pay(mesh, rows // mesh.shape["expert"], top, width, w_in.shape[2])
         body = jax.shard_map(
             local_fused if fused else local_slots,
             mesh=mesh, in_specs=in_specs, out_specs=out_specs, check_vma=False,

time: 139 us -> 123 us (0.88)
  local copies, waits for them, and re-layouts: 7.79 us -> 0 us
  Pallas kernels: 126 us -> 120 us
  other arithmetic: 1.98 us -> 0 us
    pallas_call x1, Pallas kernels: 126 us -> 115 us  [local_fused(): pl.pallas_call(functools.partial(fused_kernel, n, cap), out_shape=(jax.Sh...]
    unnamed x6 -> x0, local copies, waits for them, and re-layouts: 7.79 us -> none
    pallas_call x0 -> x1, Pallas kernels: none -> 4.57 us  [settle(): pl.pallas_call(functools.partial(copy_kernel, count), out_shape=[jax.Shap...]
where the time goes in v2:
time: 123 us; the launch traced here: 121 us
  Pallas kernels  120 us (98%)
    pallas_call x1, Pallas kernels, local_fused(): pl.pallas_call(functools.partial(fused_kernel, n, cap), out_shape=(jax.Sh...  115 us
    pallas_call x1, Pallas kernels, settle(): pl.pallas_call(functools.partial(copy_kernel, count), out_shape=[jax.Shap...  4.57 us

profile of v2, /device:TPU:13, one launch (start us, length us, event | category | flops | bytes accessed | tf_op | source)
XLA Modules:
  0.0 120.6 jit_solution(9309419382140598621)
XLA Ops:
  0.6 115.3 %fused_experts.1 = (bf16[128,1280]{1,0:T(8,128)(2,1)}, bf16[128,1280]{1,0:T(8,128)(2,1)}, bf16[1280,768]{1,0:T(8,128)(2,1)}, bf16[768,1280]{1,0:T(8,128)(2,1)}) custom-call(bf16[128,1280]{1,0:T(8,128)(2,1)} %x_ref.1, bf16[128,1280]{1,0:T(8,128)(2,1)} %dy_ref.1, s32[6,128]{1,0:T(8,128)} %bitcast.8, f32[6,128]{1,0:T(8,128)} %bitcast.9, ...), custom_call_target="tpu_custom_call" | custom-call | tf_op jit(solution)/shard_map/fused_experts/pallas_call | solution.py:468
  115.9 4.6 %settle.1 = (bf16[128,1280]{1,0:T(8,128)(2,1)}, bf16[128,1280]{1,0:T(8,128)(2,1)}, bf16[1280,768]{1,0:T(8,128)(2,1)}, bf16[768,1280]{1,0:T(8,128)(2,1)}) custom-call(bf16[128,1280]{1,0:T(8,128)(2,1)} %get-tuple-element.12.refs_0_, bf16[128,1280]{1,0:T(8,128)(2,1)} %get-tuple-element.13.refs_1_, bf16[1280,768]{1,0:T(8,128)(2,1)} %get-tuple-element.14.refs_2_, ...), custom_call_target="tpu_custom_call" | custom-call | tf_op jit(solution)/shard_map/settle/pallas_call | solution.py:446

commit v3 on v2

--- a/solution.py
+++ b/solution.py
@@ -159,6 +159,7 @@
         )
 
     pending = []
+    order = [[0]] + [[(n - h) % n, h] for h in range(1, half)] + [[half]]
 
     def off(d, h):
         return (-h if d == 0 else h) % n
@@ -206,7 +207,7 @@
             go(meta_ring(d, 1))
         go(meta_sib(0))
 
-    def hop(t, h):
+    def hop(t, h, between=None):
         if t == 0:
             for d in (0, 1):
                 if h < half or d == 0:
@@ -215,6 +216,8 @@
                         go(meta_ring(d, h + 1))
                     go(meta_sib(off(d, h)))
         for c in (0, 1):
+            if c == 1 and between is not None:
+                between()
             for d in (0, 1):
                 if c in chunks_at(d, h):
                     ring_copy(t, d, h, c).wait_recv()
@@ -318,15 +321,14 @@
             rs_s.at[t, d, h - 1, c], rs_r.at[t, d, h - 1, c], ring_to[d],
         )
 
-    def rs_hop(t, h):
+    def rs_hop(t, h, group):
         s_buf, r_buf = ((rso_s, rso_r), (rsb_s, rsb_r))[t]
-        for o in {off(1, h), off(0, h)}:
-            cat_copy(t, o).wait_recv()
-        for late in (0, 1):
-            for d in (0, 1):
-                c = d if late else 1 - d
-                if c not in chunks_at(d, h):
-                    continue
+        if h == half or group == 0:
+            for o in order[h]:
+                cat_copy(t, o).wait_recv()
+        for d in (0, 1):
+            c = d if group else 1 - d
+            if c in chunks_at(d, h):
                 rows = pl.ds(c * hrow, hrow)
                 total = contribution(t, off(1 - d, h), c)
                 if h < half and c in chunks_at(d, h + 1):
@@ -365,12 +367,6 @@
     stores = []
     tile = 256
     n_out, n_in = act.shape[1] // tile, rows_x.shape[1] // tile
-
-    def part(count, h):
-        k = half - 1 - h
-        return range(count * k // (half - 1), count * (k + 1) // (half - 1))
-
-    order = [[0]] + [[off(0, h), off(1, h)] for h in range(1, half)] + [[half]]
 
     def each(f, i):
         for o in order[i]:
@@ -389,32 +385,38 @@
     hop(0, half)
     take_x(half)
     for h in range(1, half - 1):
-        hop(1, h)
-        each(take_dy, h - 1)
+        hop(1, h, lambda: each(take_dy, h - 1))
         each(forward, h - 1)
-    hop(1, half - 1)
+    hop(1, half - 1, lambda: each(forward, half))
+    rs_hop(0, half, 1)
     each(take_dy, half - 2)
-    each(forward, half - 2)
-    each(forward, half)
     each(forward, half - 1)
-    rs_hop(0, half)
+    rs_hop(0, half - 1, 0)
     hop(1, half)
     each(take_dy, half - 1)
-    rs_hop(0, half - 1)
-    each(take_dy, half)
-    each(backward, 0)
-    out_tiles(part(n_out, half - 1))
-    for h in range(half - 2, 0, -1):
-        rs_hop(0, h)
-        each(backward, half - 1 - h)
-        out_tiles(part(n_out, h))
+    rs_hop(0, half - 1, 1)
+    each(forward, half - 2)
+    fill = [lambda: each(take_dy, half)]
+    for i in range(half - 1):
+        fill += [functools.partial(backward, o) for o in order[i]]
+    fill += [functools.partial(out_tiles, [i]) for i in range(n_out - 1)]
+    steps = [(h, g) for h in range(half - 2, 0, -1) for g in (0, 1)]
+
+    def spread(t, steps, fill):
+        for i, (h, g) in enumerate(steps):
+            rs_hop(t, h, g)
+            for f in fill[len(fill) * i // len(steps):len(fill) * (i + 1) // len(steps)]:
+                f()
+
+    spread(0, steps, fill)
+    each(backward, half)
+    rs_hop(1, half, 1)
     each(backward, half - 1)
-    each(backward, half)
-    rs_hop(1, half)
+    rs_hop(1, half - 1, 0)
     rs_last(0)
-    for h in range(half - 1, 0, -1):
-        rs_hop(1, h)
-        in_tiles(part(n_in, h))
+    fill = [functools.partial(in_tiles, [i]) for i in range(n_in)]
+    fill += [functools.partial(out_tiles, [n_out - 1])]
+    spread(1, [(half - 1, 1)] + steps, fill)
     rs_last(1)
     for copy in stores:
         copy.wait()

time: 123 us -> 121 us (0.984)
  Pallas kernels: 120 us -> 118 us
    pallas_call x1, Pallas kernels: 115 us -> 114 us  [local_fused(): pl.pallas_call(functools.partial(fused_kernel, n, cap), out_shape=(jax.Sh...]
where the time goes in v3:
time: 121 us; the launch traced here: 119 us
  Pallas kernels  118 us (98%)
    pallas_call x1, Pallas kernels, local_fused(): pl.pallas_call(functools.partial(fused_kernel, n, cap), out_shape=(jax.Sh...  114 us
    pallas_call x1, Pallas kernels, settle(): pl.pallas_call(functools.partial(copy_kernel, count), out_shape=[jax.Shap...  4.57 us

profile of v3, /device:TPU:13, one launch (start us, length us, event | category | flops | bytes accessed | tf_op | source)
XLA Modules:
  0.0 119.0 jit_solution(16747889789194667339)
XLA Ops:
  0.6 113.6 %fused_experts.1 = (bf16[128,1280]{1,0:T(8,128)(2,1)}, bf16[128,1280]{1,0:T(8,128)(2,1)}, bf16[1280,768]{1,0:T(8,128)(2,1)}, bf16[768,1280]{1,0:T(8,128)(2,1)}) custom-call(bf16[128,1280]{1,0:T(8,128)(2,1)} %x_ref.1, bf16[128,1280]{1,0:T(8,128)(2,1)} %dy_ref.1, s32[6,128]{1,0:T(8,128)} %bitcast.8, f32[6,128]{1,0:T(8,128)} %bitcast.9, ...), custom_call_target="tpu_custom_call" | custom-call | tf_op jit(solution)/shard_map/fused_experts/pallas_call | solution.py:470
  114.2 4.6 %settle.1 = (bf16[128,1280]{1,0:T(8,128)(2,1)}, bf16[128,1280]{1,0:T(8,128)(2,1)}, bf16[1280,768]{1,0:T(8,128)(2,1)}, bf16[768,1280]{1,0:T(8,128)(2,1)}) custom-call(bf16[128,1280]{1,0:T(8,128)(2,1)} %get-tuple-element.12.refs_0_, bf16[128,1280]{1,0:T(8,128)(2,1)} %get-tuple-element.13.refs_1_, bf16[1280,768]{1,0:T(8,128)(2,1)} %get-tuple-element.14.refs_2_, ...), custom_call_target="tpu_custom_call" | custom-call | tf_op jit(solution)/shard_map/settle/pallas_call | solution.py:448
